TPU v7x, 32 devices: a whole 2x2x4 slice. The times are simulated.
32 devices in a mesh: tile: 16 (over z, y, x), band: 2 (over core).
Axes of the slice: x: 2, y: 2, z: 4, core: 2. Of those that a mesh axis runs over, the one named last changes fastest.
Arguments:
- voxel_feat: bfloat16 [4096, 64, 256], P(('tile', 'band')), may hold values from -6 to 6
- window_count: int32 [4096], P(('tile', 'band')), may hold values from 1 to 64
- voxel_cell: int32 [4096, 64], P(('tile', 'band')), may hold values from 0 to 2047
- w_qkv_voxel: bfloat16 [256, 768], replicated, may hold values from -1 to 1
- w_out_voxel: bfloat16 [256, 256], replicated, may hold values from -0.375 to 0.375
- w_up_voxel: bfloat16 [256, 512], replicated, may hold values from -0.375 to 0.375
- w_down_voxel: bfloat16 [512, 256], replicated, may hold values from -0.25 to 0.25
- conv_taps: float32 [9, 256], replicated, may hold values from -2 to 2
- w_qkv_bev: bfloat16 [256, 768], replicated, may hold values from -1 to 1
- w_out_bev: bfloat16 [256, 256], replicated, may hold values from -0.375 to 0.375
- w_up_bev: bfloat16 [256, 512], replicated, may hold values from -0.375 to 0.375
- w_down_bev: bfloat16 [512, 256], replicated, may hold values from -0.25 to 0.25
Outputs:
- bev_out: bfloat16 [256, 128, 256], P(('tile', 'band'))
Inputs may be any that keep to these rules, and one draw needn't show every extreme that they name: The live slots of a window are its first window_count slots. `voxel_cell`: read only for live slots.
All inputs are finite; a program needn't handle non-finite values.
Results may differ from a plain program's by a relative error of at most 0.035.
Values may be sent and summed in bfloat16 or wider, within the bound.
A program may use at most 192 MiB of HBM per device.

v0:
```python
import functools
import math

import jax
import jax.numpy as jnp
from jax import lax
from jax.experimental import pallas as pl
from jax.experimental.pallas import tpu as pltpu
from jax.sharding import PartitionSpec as P

HEADS = 8
WSIDE = 8
CB = 8
LANES = 128


def swapped(x, axis, bit):
    return lax.ppermute(x, axis, [(i, i ^ 1 << bit) for i in range(lax.axis_size(axis))])


def with_halo(block, sides, width):
    for axis, dim in sides:
        count = lax.axis_size(axis)
        forward = [(i, i + 1) for i in range(count - 1)]
        backward = [(target, source) for source, target in forward]
        low = lax.ppermute(
            lax.slice_in_dim(block, block.shape[dim] - width, None, axis=dim), axis, forward
        )
        high = lax.ppermute(lax.slice_in_dim(block, 0, width, axis=dim), axis, backward)
        block = jnp.concatenate([low, block, high], axis=dim)
    return block


def layer_norm(values, axis=-1):
    center = values - jnp.mean(values, axis=axis, keepdims=True)
    spread = jnp.mean(center * center, axis=axis, keepdims=True)
    return center * lax.rsqrt(spread + 1e-05)


def dot(a, b, contract=(1, 0)):
    return lax.dot_general(
        a, b, (((contract[0],), (contract[1],)), ((), ())), preferred_element_type=jnp.float32
    )


def attend_columns(x, counts, w_qv, w_k, w_out, w_up, w_down):
    tokens, width = x.shape
    head_dim = width // HEADS
    half_heads = LANES // head_dim
    slots = LANES // 2
    factor = head_dim ** (-0.5) * math.log2(math.e)
    turned = dot(w_qv, x, (1, 1))
    queries = turned[:width].astype(jnp.bfloat16)
    vals = turned[width:]
    keys = dot(x, w_k).astype(jnp.bfloat16)
    lane = lax.broadcasted_iota(jnp.int32, (LANES, LANES), 1)
    row = lax.broadcasted_iota(jnp.int32, (LANES, LANES), 0)
    first = lane < slots
    first_b = first.astype(jnp.bfloat16)
    second_b = 1 - first_b
    key_head = lane[:slots] // head_dim
    key_masks = [(key_head == h).astype(jnp.bfloat16) for h in range(half_heads)]
    val_masks = [
        (row // head_dim == 2 * j + lane // slots).astype(jnp.bfloat16)
        for j in range(half_heads // 2)
    ]
    mixed = []
    for pair in range(tokens // LANES):
        at = pair * LANES
        if counts is not None:
            limit = jnp.where(first[:slots], counts(2 * pair), counts(2 * pair + 1))
            bias = jnp.where(row[:slots] < limit, 0.0, -1e30)
        halves = []
        for half in range(width // LANES):
            f = half * LANES
            q = queries[f : f + LANES, at : at + LANES]
            q_blocks = jnp.concatenate([q * first_b, q * second_b], axis=0)
            k_blocks = jnp.concatenate(
                [
                    jnp.concatenate(
                        [
                            keys[at + w * slots : at + (w + 1) * slots, f : f + LANES] * m
                            for m in key_masks
                        ],
                        axis=0,
                    )
                    for w in range(2)
                ],
                axis=1,
            )
            scores = dot(k_blocks, q_blocks).reshape(half_heads, slots, LANES)
            if counts is not None:
                scores = scores + bias[None]
            top = jnp.max(scores, axis=1, keepdims=True)
            raised = jnp.exp2((scores - top) * factor)
            total = jnp.sum(raised, axis=1, keepdims=True)
            weights = raised.astype(jnp.bfloat16).reshape(half_heads * slots, LANES)
            v = vals[f : f + LANES, at : at + LANES]
            rolled = pltpu.roll(v, slots, 1)
            v_blocks = []
            for w in range(2):
                twice = (jnp.where(first, v, rolled) if w == 0 else jnp.where(first, rolled, v))
                twice = twice.astype(jnp.bfloat16)
                v_blocks.append(jnp.concatenate([twice * m for m in val_masks], axis=1))
            out = dot(jnp.concatenate(v_blocks, axis=0), weights)
            out = jnp.where(first, out[:LANES], out[LANES:])
            out = out.reshape(half_heads, head_dim, LANES) / total
            halves.append(out.reshape(LANES, LANES).astype(jnp.bfloat16))
        mixed.append(jnp.concatenate(halves, axis=0))
    mixed = jnp.concatenate(mixed, axis=1)
    projected = dot(w_out, mixed)
    hidden = layer_norm(x.astype(jnp.float32).T + projected, 0).astype(jnp.bfloat16)
    lifted = jax.nn.relu(dot(w_up, hidden)).astype(jnp.bfloat16)
    lowered = dot(w_down, lifted)
    return layer_norm(hidden.astype(jnp.float32) + lowered, 0)


def voxel_kernel(
    count_ref, x_ref, cell_ref, qv_ref, k_ref, out_ref, up_ref, down_ref, pooled_ref, acc, enc
):
    step = pl.program_id(0)
    per_step = x_ref.shape[0] * 2 // LANES

    @pl.when(step == 0)
    def _():
        acc[...] = jnp.zeros_like(acc)

    enc[...] = attend_columns(
        x_ref[...],
        lambda w: count_ref[step * per_step + w],
        qv_ref[...],
        k_ref[...],
        out_ref[...],
        up_ref[...],
        down_ref[...],
    ).astype(jnp.bfloat16)
    block = 2 * LANES
    row = lax.broadcasted_iota(jnp.int32, (block, x_ref.shape[0]), 0)

    def pool(i, carry):
        at = pl.multiple_of(i * block, block)
        hot = jnp.where(row == cell_ref[0] - at, 1.0, 0.0).astype(jnp.bfloat16)
        acc[pl.ds(at, block), :] += dot(hot, enc[...], (1, 1))
        return carry

    lax.fori_loop(0, acc.shape[0] // block, pool, 0)

    @pl.when(step == pl.num_programs(0) - 1)
    def _():
        pooled_ref[...] = acc[...].astype(jnp.bfloat16)


def whole(array):
    return pl.BlockSpec(array.shape, lambda *_: (0,) * array.ndim)


def turned_weights(w_qkv, w_out, w_up, w_down):
    width = w_out.shape[0]
    w_qv = jnp.concatenate([w_qkv[:, :width], w_qkv[:, 2 * width :]], axis=1).T
    return w_qv, w_qkv[:, width : 2 * width], w_out.T, w_up.T, w_down.T


def voxel_pool(feat, counts, target, cells, weights):
    tokens, width = feat.shape
    size = min(512, tokens)
    steps = tokens // size
    return pl.pallas_call(
        voxel_kernel,
        grid_spec=pltpu.PrefetchScalarGridSpec(
            num_scalar_prefetch=1,
            grid=(steps,),
            in_specs=[
                pl.BlockSpec((size, width), lambda i, c: (i, 0)),
                pl.BlockSpec((1, 1, size), lambda i, c: (i, 0, 0)),
            ]
            + [whole(w) for w in weights],
            out_specs=pl.BlockSpec((cells, width), lambda i, c: (0, 0)),
            scratch_shapes=[
                pltpu.VMEM((cells, width), jnp.float32),
                pltpu.VMEM((width, size), jnp.bfloat16),
            ],
        ),
        out_shape=jax.ShapeDtypeStruct((cells, width), jnp.bfloat16),
        name="voxel_pool",
    )(counts, feat, target.reshape(steps, 1, size), *weights)


def bev_kernel(x_ref, qv_ref, k_ref, out_ref, up_ref, down_ref, result_ref):
    result_ref[...] = attend_columns(
        x_ref[...], None, qv_ref[...], k_ref[...], out_ref[...], up_ref[...], down_ref[...]
    ).T.astype(jnp.bfloat16)


def bev_block(x, weights):
    tokens, width = x.shape
    size = min(512, tokens)
    return pl.pallas_call(
        bev_kernel,
        grid=(tokens // size,),
        in_specs=[pl.BlockSpec((size, width), lambda i: (i, 0))] + [whole(w) for w in weights],
        out_specs=pl.BlockSpec((size, width), lambda i: (i, 0)),
        out_shape=jax.ShapeDtypeStruct(x.shape, jnp.bfloat16),
        name="bev_block",
    )(x, *weights)


def shards(
    voxel_feat,
    window_count,
    voxel_cell,
    w_qkv_voxel,
    w_out_voxel,
    w_up_voxel,
    w_down_voxel,
    conv_taps,
    w_qkv_bev,
    w_out_bev,
    w_up_bev,
    w_down_bev,
):
    n_tile = lax.axis_size("tile")
    n_band = lax.axis_size("band")
    rows = WSIDE * n_tile * n_band
    cols = CB * n_tile
    width = voxel_feat.shape[2]
    slot_ids = jnp.arange(voxel_feat.shape[1], dtype=jnp.int32)
    keep = slot_ids[None, :] < window_count[:, None]
    target = jnp.where(keep, voxel_cell, -1)
    partial_value = voxel_pool(
        voxel_feat.reshape(-1, width),
        window_count,
        target,
        rows * CB,
        turned_weights(w_qkv_voxel, w_out_voxel, w_up_voxel, w_down_voxel),
    )
    split_rows = partial_value.reshape(n_tile, n_band, WSIDE, CB, width)
    band = lax.axis_index("band")
    mine = lax.dynamic_index_in_dim(split_rows, band, 1, keepdims=False)
    others = lax.dynamic_index_in_dim(split_rows, 1 - band, 1, keepdims=False)
    received = swapped(others, "band", 0)
    strip_part = layer_norm(mine.astype(jnp.float32) + received.astype(jnp.float32)).astype(
        jnp.bfloat16
    )
    arrived = lax.all_to_all(strip_part, "tile", split_axis=0, concat_axis=2, tiled=True)
    bev = arrived.reshape(WSIDE, cols, width)
    extended = with_halo(bev, ((("tile", "band"), 0),), 1)
    padded = jnp.pad(extended, ((0, 0), (1, 1), (0, 0)))
    position = jnp.zeros((WSIDE, cols, width), jnp.float32)
    for row_tap in range(3):
        for col_tap in range(3):
            position = (
                position
                + padded[row_tap : row_tap + WSIDE, col_tap : col_tap + cols].astype(jnp.float32)
                * conv_taps[3 * row_tap + col_tap]
            )
    shaped = (bev.astype(jnp.float32) + position).astype(jnp.bfloat16)
    across = cols // WSIDE
    windows = (
        shaped.reshape(WSIDE, across, WSIDE, width)
        .transpose(1, 0, 2, 3)
        .reshape(across * WSIDE * WSIDE, width)
    )
    result = bev_block(windows, turned_weights(w_qkv_bev, w_out_bev, w_up_bev, w_down_bev))
    return (
        result.reshape(across, WSIDE, WSIDE, width)
        .transpose(1, 0, 2, 3)
        .reshape(WSIDE, cols, width)
    )


def solution(mesh):
    placed = (
        P(("tile", "band"), None, None),
        P(("tile", "band")),
        P(("tile", "band"), None),
        P(),
        P(),
        P(),
        P(),
        P(),
        P(),
        P(),
        P(),
        P(),
    )
    return jax.shard_map(
        shards,
        mesh=mesh,
        in_specs=placed,
        out_specs=P(("tile", "band"), None, None),
        check_vma=False,
    )
```

profile of v0, /device:TPU:1, one launch (start us, length us, event | category | flops | bytes accessed | tf_op | source)
XLA Modules:
  0.0 125.0 jit_solution(5605866563776814745)
XLA Ops:
  0.0 1.8 %fusion.17 = (bf16[256,256]{1,0:T(8,128)(2,1)}, bf16[256,256]{1,0:T(8,128)(2,1)S(1)}, bf16[256,256]{1,0:T(8,128)(2,1)S(1)}) fusion(bf16[256,768]{1,0:T(8,128)(2,1)} %param.15), kind=kLoop, calls=%fused_computation.37 | loop fusion | bytes 786432 | tf_op jit(solution)/shard_map/slice | solution.py:160
  2.0 0.9 copy.45
  2.9 0.9 copy.46
  3.7 0.8 copy.44
  4.6 0.7 reshape.60.cell_ref
  5.3 0.7 maximum_bitcast_fusion.qv_ref
  6.1 72.1 %voxel_pool.1 = bf16[2048,256]{1,0:T(8,128)(2,1)} custom-call(s32[128]{0:T(128)} %count_ref.1, bf16[8192,256]{1,0:T(8,128)(2,1)} %bitcast.60, s32[16,1,512]{2,1,0:T(1,128)} %reshape.60.cell_ref, bf16[512,256]{1,0:T(8,128)(2,1)} %maximum_bitcast_fusion.qv_ref, bf16[256,256]{1,0:T(8,128)(2,1)} %get-tuple-element.12.k_ref, bf16[256,256]{1,0:T(8,128)(2,1)} %bitcast.68, ...), custom_call_target="tpu_custom_call" | custom-call | tf_op jit(solution)/shard_map/voxel_pool/pallas_call | solution.py:167
  78.2 1.2 dynamic-slice_bitcast_fusion
  79.4 1.9 %collective-permute-done = bf16[16,8,8,256]{3,2,1,0:T(8,128)(2,1)S(1)} collective-permute-done((bf16[16,8,8,256]{3,2,1,0:T(8,128)(2,1)S(1)}, bf16[16,8,8,256]{3,2,1,0:T(8,128)(2,1)S(1)}, u32[]{:S(2)}, u32[]{:S(2)}) %collective-permute-start) | collective-permute-done | bytes 524320 | tf_op jit(solution)/shard_map/ppermute | solution.py:18
  82.0 1.1 multiply_convert_fusion
  83.2 7.8 %all-to-all-start = ((bf16[16,8,8,256]{3,2,1,0:T(8,128)(2,1)}), bf16[16,8,8,256]{3,2,1,0:T(8,128)(2,1)S(1)}, u32[]{:S(2)}, u32[]{:S(2)}) async-start(bf16[16,8,8,256]{3,2,1,0:T(8,128)(2,1)} %multiply_convert_fusion), calls=%async_computation | async-start | bytes 1048576 | tf_op jit(solution)/shard_map/all_to_all | solution.py:244
  91.0 0.7 fusion.16
  91.9 0.9 copy.54
  92.8 0.9 copy.55
  93.7 0.8 copy.53
  94.4 9.2 %all-to-all-done = bf16[16,8,8,256]{3,2,1,0:T(8,128)(2,1)S(1)} async-done(((bf16[16,8,8,256]{3,2,1,0:T(8,128)(2,1)}), bf16[16,8,8,256]{3,2,1,0:T(8,128)(2,1)S(1)}, u32[]{:S(2)}, u32[]{:S(2)}) %all-to-all-start) | async-done | bytes 524320 | tf_op jit(solution)/shard_map/all_to_all | solution.py:244
  103.7 5.5 %collective-permute-start.1 = (bf16[1,128,256]{2,1,0:T(8,128)(2,1)S(1)}, bf16[1,128,256]{2,1,0:T(8,128)(2,1)S(1)}, u32[]{:S(2)}, u32[]{:S(2)}) collective-permute-start(bf16[1,128,256]{2,1,0:T(8,128)(2,1)S(1)} %get-tuple-element.5), channel_id=1, source_target_pairs={{0,1},{1,2},{2,3},{3,4},{4,5},{5,6},{6,7},{7,8},{8,9},{9,10},{10,1... | collective-permute-start | bytes 196616 | tf_op jit(solution)/shard_map/ppermute | solution.py:26
  109.2 1.9 %collective-permute-start.2 = (bf16[1,128,256]{2,1,0:T(8,128)(2,1)S(1)}, bf16[1,128,256]{2,1,0:T(8,128)(2,1)S(1)}, u32[]{:S(2)}, u32[]{:S(2)}) collective-permute-start(bf16[1,128,256]{2,1,0:T(8,128)(2,1)S(1)} %get-tuple-element.6), channel_id=1, source_target_pairs={{1,0},{2,1},{3,2},{4,3},{5,4},{6,5},{7,6},{8,7},{9,8},{10,9},{11,1... | collective-permute-start | bytes 196616 | tf_op jit(solution)/shard_map/ppermute | solution.py:29
  111.1 0.7 maximum_bitcast_fusion.1.qv_ref
  111.9 2.9 %collective-permute-done.2 = bf16[1,128,256]{2,1,0:T(8,128)(2,1)S(1)} collective-permute-done((bf16[1,128,256]{2,1,0:T(8,128)(2,1)S(1)}, bf16[1,128,256]{2,1,0:T(8,128)(2,1)S(1)}, u32[]{:S(2)}, u32[]{:S(2)}) %collective-permute-start.2) | collective-permute-done | bytes 65568 | tf_op jit(solution)/shard_map/ppermute | solution.py:29
  115.0 0.8 fusion.14
  115.8 0.8 copy.50
  116.6 6.5 %bev_block.1 = bf16[1024,256]{1,0:T(8,128)(2,1)} custom-call(bf16[1024,256]{1,0:T(8,128)(2,1)} %bitcast.61, bf16[512,256]{1,0:T(8,128)(2,1)} %maximum_bitcast_fusion.1.qv_ref, bf16[256,256]{1,0:T(8,128)(2,1)} %get-tuple-element.9.k_ref, bf16[256,256]{1,0:T(8,128)(2,1)} %bitcast.67, bf16[512,256]{1,0:T(8,128)(2,1)} %bitcast.65, bf16[256,512]{1,0:T(8,128)(2,1)} %bitcast.66), custom_call_target="tpu_custom_call" | custom-call | tf_op jit(solution)/shard_map/bev_block/pallas_call | solution.py:197
  123.1 1.9 %copy.65 = bf16[8,16,8,256]{3,2,1,0:T(8,128)(2,1)} copy(bf16[8,16,8,256]{3,2,0,1:T(8,128)(2,1)} %bitcast.62) | data formatting | bytes 1048576 | tf_op jit(solution)/shard_map/transpose | solution.py:266
  (38 shorter events, 1.5 us)
Async XLA Ops:
  0.0 2.0 %copy-start.2 = (bf16[256,512]{1,0:T(8,128)(2,1)S(1)}, bf16[256,512]{1,0:T(8,128)(2,1)}, u32[]{:S(2)}) copy-start(bf16[256,512]{1,0:T(8,128)(2,1)} %param.17) | copy-start | bytes 786436
  0.0 2.9 %copy-start.3 = (bf16[512,256]{1,0:T(8,128)(2,1)S(1)}, bf16[512,256]{1,0:T(8,128)(2,1)}, u32[]{:S(2)}) copy-start(bf16[512,256]{1,0:T(8,128)(2,1)} %param.18) | copy-start | bytes 786436
  0.0 3.7 %copy-start.6 = (bf16[256,256]{1,0:T(8,128)(2,1)S(1)}, bf16[256,256]{1,0:T(8,128)(2,1)}, u32[]{:S(2)}) copy-start(bf16[256,256]{1,0:T(8,128)(2,1)} %param.16) | copy-start | bytes 393220
  0.0 4.5 %copy-start.10 = (s32[128]{0:T(128)S(1)}, s32[128]{0:T(128)}, u32[]{:S(2)}) copy-start(s32[128]{0:T(128)} %count_ref.1) | copy-start | bytes 1540
  0.0 4.5 %copy-start.8 = (s32[128,64]{0,1:T(8,128)S(1)}, s32[128,64]{0,1:T(8,128)}, u32[]{:S(2)}) copy-start(s32[128,64]{0,1:T(8,128)} %param.14) | copy-start | bytes 98308
  78.2 3.1 %copy-start = (bf16[2048,256]{1,0:T(8,128)(2,1)S(1)}, bf16[2048,256]{1,0:T(8,128)(2,1)}, u32[]{:S(2)}) copy-start(bf16[2048,256]{1,0:T(8,128)(2,1)} %voxel_pool.1) | copy-start | bytes 3145732
  79.4 2.0 %collective-permute-start = (bf16[16,8,8,256]{3,2,1,0:T(8,128)(2,1)S(1)}, bf16[16,8,8,256]{3,2,1,0:T(8,128)(2,1)S(1)}, u32[]{:S(2)}, u32[]{:S(2)}) collective-permute-start(bf16[16,8,8,256]{3,2,1,0:T(8,128)(2,1)S(1)} %dynamic-slice_bitcast_fusion), channel_id=1, source_target_pairs={{0,1},{1,0},{2,3},{3,2},{4,5},{5,4},{6,7},{7,6},{8,9},{9,8},{10,11... | collective-permute-start | bytes 1572872 | tf_op jit(solution)/shard_map/ppermute | solution.py:18
  82.0 9.0 %copy-start.1 = (bf16[256,768]{1,0:T(8,128)(2,1)S(1)}, bf16[256,768]{1,0:T(8,128)(2,1)}, u32[]{:S(2)}) copy-start(bf16[256,768]{1,0:T(8,128)(2,1)} %param.20) | copy-start | bytes 1179652
  83.2 8.8 %copy-start.4 = (bf16[256,512]{1,0:T(8,128)(2,1)S(1)}, bf16[256,512]{1,0:T(8,128)(2,1)}, u32[]{:S(2)}) copy-start(bf16[256,512]{1,0:T(8,128)(2,1)} %param.22) | copy-start | bytes 786436
  83.2 9.6 %copy-start.5 = (bf16[512,256]{1,0:T(8,128)(2,1)S(1)}, bf16[512,256]{1,0:T(8,128)(2,1)}, u32[]{:S(2)}) copy-start(bf16[512,256]{1,0:T(8,128)(2,1)} %param.23) | copy-start | bytes 786436
  83.2 20.5 %all-to-all-start = ((bf16[16,8,8,256]{3,2,1,0:T(8,128)(2,1)}), bf16[16,8,8,256]{3,2,1,0:T(8,128)(2,1)S(1)}, u32[]{:S(2)}, u32[]{:S(2)}) async-start(bf16[16,8,8,256]{3,2,1,0:T(8,128)(2,1)} %multiply_convert_fusion), calls=%async_computation | async-start | bytes 1048576 | tf_op jit(solution)/shard_map/all_to_all | solution.py:244
  91.0 2.7 %copy-start.7 = (bf16[256,256]{1,0:T(8,128)(2,1)S(1)}, bf16[256,256]{1,0:T(8,128)(2,1)}, u32[]{:S(2)}) copy-start(bf16[256,256]{1,0:T(8,128)(2,1)} %param.21) | copy-start | bytes 393220
  91.0 3.4 %copy-start.9 = (f32[9,256]{1,0:T(8,128)S(1)}, f32[9,256]{1,0:T(8,128)}, u32[]{:S(2)}) copy-start(f32[9,256]{1,0:T(8,128)} %param.19) | copy-start | bytes 27652
  103.7 8.2 %collective-permute-start.1 = (bf16[1,128,256]{2,1,0:T(8,128)(2,1)S(1)}, bf16[1,128,256]{2,1,0:T(8,128)(2,1)S(1)}, u32[]{:S(2)}, u32[]{:S(2)}) collective-permute-start(bf16[1,128,256]{2,1,0:T(8,128)(2,1)S(1)} %get-tuple-element.5), channel_id=1, source_target_pairs={{0,1},{1,2},{2,3},{3,4},{4,5},{5,6},{6,7},{7,8},{8,9},{9,10},{10,1... | collective-permute-start | bytes 196616 | tf_op jit(solution)/shard_map/ppermute | solution.py:26
  109.2 5.6 %collective-permute-start.2 = (bf16[1,128,256]{2,1,0:T(8,128)(2,1)S(1)}, bf16[1,128,256]{2,1,0:T(8,128)(2,1)S(1)}, u32[]{:S(2)}, u32[]{:S(2)}) collective-permute-start(bf16[1,128,256]{2,1,0:T(8,128)(2,1)S(1)} %get-tuple-element.6), channel_id=1, source_target_pairs={{1,0},{2,1},{3,2},{4,3},{5,4},{6,5},{7,6},{8,7},{9,8},{10,9},{11,1... | collective-permute-start | bytes 196616 | tf_op jit(solution)/shard_map/ppermute | solution.py:29
where the time goes:
time: 127 us; the launch traced here: 125 us
  Pallas kernels  78.6 us (62%)
  starting transfers between devices  15.3 us (12%)
  waiting for transfers between devices  14 us (11%)
  local copies, waits for them, and re-layouts  12.6 us (10%)
  other arithmetic  4.25 us (3%)
    pallas_call x1, Pallas kernels, voxel_pool(): pl.pallas_call(voxel_kernel, grid_spec=pltpu.PrefetchScalarGridSpec(num_s...  72.1 us
    all_to_all x1, waiting for transfers between devices, shards(): lax.all_to_all(strip_part, 'tile', split_axis=0, concat_axis=2, tiled=True)  9.19 us
    all_to_all x1, starting transfers between devices, shards(): lax.all_to_all(strip_part, 'tile', split_axis=0, concat_axis=2, tiled=True)  7.83 us
    pallas_call x1, Pallas kernels, bev_block(): pl.pallas_call(bev_kernel, grid=(tokens // size,), in_specs=[pl.BlockSpec...  6.48 us
    ppermute x1, starting transfers between devices, with_halo(): lax.ppermute(lax.slice_in_dim(block, block.shape[dim] - width, None, axis...  5.49 us
    unnamed x32, local copies, waits for them, and re-layouts  5.41 us
    ppermute x1, waiting for transfers between devices, with_halo(): lax.ppermute(lax.slice_in_dim(block, 0, width, axis=dim), axis, backward)  2.92 us
  transfers between devices with their start and end apart: 4, of which 3 were waited for; matrix products, arithmetic and copies ran while one was open for 3% of the time, Pallas kernels for 0%

commit v1 on v0

v1 whole, which is shorter than its diff:
```python
import functools
import math

import jax
import jax.numpy as jnp
from jax import lax
from jax.experimental import pallas as pl
from jax.experimental.pallas import tpu as pltpu
from jax.sharding import PartitionSpec as P

HEADS = 8
WSIDE = 8
CB = 8
LANES = 128


def layer_norm(values, axis=-1):
    center = values - jnp.mean(values, axis=axis, keepdims=True)
    spread = jnp.mean(center * center, axis=axis, keepdims=True)
    return center * lax.rsqrt(spread + 1e-05)


def dot(a, b, contract=(1, 0)):
    return lax.dot_general(
        a, b, (((contract[0],), (contract[1],)), ((), ())), preferred_element_type=jnp.float32
    )


def attend_columns(x, counts, w_qv, w_k, w_out, w_up, w_down):
    tokens, width = x.shape
    head_dim = width // HEADS
    half_heads = LANES // head_dim
    slots = LANES // 2
    factor = head_dim ** (-0.5) * math.log2(math.e)
    turned = dot(w_qv, x, (1, 1))
    queries = turned[:width].astype(jnp.bfloat16)
    vals = turned[width:]
    keys = dot(x, w_k).astype(jnp.bfloat16)
    lane = lax.broadcasted_iota(jnp.int32, (LANES, LANES), 1)
    row = lax.broadcasted_iota(jnp.int32, (LANES, LANES), 0)
    first = lane < slots
    first_b = first.astype(jnp.bfloat16)
    second_b = 1 - first_b
    key_head = lane[:slots] // head_dim
    key_masks = [(key_head == h).astype(jnp.bfloat16) for h in range(half_heads)]
    val_masks = [
        (row // head_dim == 2 * j + lane // slots).astype(jnp.bfloat16)
        for j in range(half_heads // 2)
    ]
    mixed = []
    for pair in range(tokens // LANES):
        at = pair * LANES
        if counts is not None:
            limit = jnp.where(first[:slots], counts(2 * pair), counts(2 * pair + 1))
            bias = jnp.where(row[:slots] < limit, 0.0, -1e30)
        halves = []
        for half in range(width // LANES):
            f = half * LANES
            q = queries[f : f + LANES, at : at + LANES]
            q_blocks = jnp.concatenate([q * first_b, q * second_b], axis=0)
            k_blocks = jnp.concatenate(
                [
                    jnp.concatenate(
                        [
                            keys[at + w * slots : at + (w + 1) * slots, f : f + LANES] * m
                            for m in key_masks
                        ],
                        axis=0,
                    )
                    for w in range(2)
                ],
                axis=1,
            )
            scores = dot(k_blocks, q_blocks).reshape(half_heads, slots, LANES)
            if counts is not None:
                scores = scores + bias[None]
            top = jnp.max(scores, axis=1, keepdims=True)
            raised = jnp.exp2((scores - top) * factor)
            total = jnp.sum(raised, axis=1, keepdims=True)
            weights = raised.astype(jnp.bfloat16).reshape(half_heads * slots, LANES)
            v = vals[f : f + LANES, at : at + LANES]
            rolled = pltpu.roll(v, slots, 1)
            v_blocks = []
            for w in range(2):
                twice = (jnp.where(first, v, rolled) if w == 0 else jnp.where(first, rolled, v))
                twice = twice.astype(jnp.bfloat16)
                v_blocks.append(jnp.concatenate([twice * m for m in val_masks], axis=1))
            out = dot(jnp.concatenate(v_blocks, axis=0), weights)
            out = jnp.where(first, out[:LANES], out[LANES:])
            out = out.reshape(half_heads, head_dim, LANES) / total
            halves.append(out.reshape(LANES, LANES).astype(jnp.bfloat16))
        mixed.append(jnp.concatenate(halves, axis=0))
    mixed = jnp.concatenate(mixed, axis=1)
    projected = dot(w_out, mixed)
    hidden = layer_norm(x.astype(jnp.float32).T + projected, 0).astype(jnp.bfloat16)
    lifted = jax.nn.relu(dot(w_up, hidden)).astype(jnp.bfloat16)
    lowered = dot(w_down, lifted)
    return layer_norm(hidden.astype(jnp.float32) + lowered, 0)


def turn_weights(qkv_ref, out_ref, up_ref, down_ref, qv_s, out_s, up_s, down_s):
    width = out_ref.shape[0]

    def turned(values):
        return values.astype(jnp.float32).T.astype(jnp.bfloat16)

    qv_s[:width, :] = turned(qkv_ref[:, :width])
    qv_s[width:, :] = turned(qkv_ref[:, 2 * width :])
    out_s[...] = turned(out_ref[...])
    up_s[...] = turned(up_ref[...])
    down_s[...] = turned(down_ref[...])


def turned_scratch(w_qkv, w_out, w_up, w_down):
    width = w_out.shape[0]
    return [
        pltpu.VMEM((2 * width, width), jnp.bfloat16),
        pltpu.VMEM(w_out.shape[::-1], jnp.bfloat16),
        pltpu.VMEM(w_up.shape[::-1], jnp.bfloat16),
        pltpu.VMEM(w_down.shape[::-1], jnp.bfloat16),
    ]


def whole(array):
    return pl.BlockSpec(array.shape, lambda *_: (0,) * array.ndim)


def voxel_kernel(
    count_ref, x_ref, qkv_ref, out_ref, up_ref, down_ref, enc_ref, qv_s, out_s, up_s, down_s
):
    step = pl.program_id(0)
    per_step = x_ref.shape[0] * 2 // LANES
    width = x_ref.shape[1]

    @pl.when(step == 0)
    def _():
        turn_weights(qkv_ref, out_ref, up_ref, down_ref, qv_s, out_s, up_s, down_s)

    enc_ref[0] = attend_columns(
        x_ref[...],
        lambda w: count_ref[step * per_step + w],
        qv_s[...],
        qkv_ref[:, width : 2 * width],
        out_s[...],
        up_s[...],
        down_s[...],
    ).astype(jnp.bfloat16)


def voxel_block(feat, counts, weights):
    tokens, width = feat.shape
    size = min(512, tokens)
    steps = tokens // size
    return pl.pallas_call(
        voxel_kernel,
        grid_spec=pltpu.PrefetchScalarGridSpec(
            num_scalar_prefetch=1,
            grid=(steps,),
            in_specs=[pl.BlockSpec((size, width), lambda i, c: (i, 0))]
            + [whole(w) for w in weights],
            out_specs=pl.BlockSpec((1, width, size), lambda i, c: (i, 0, 0)),
            scratch_shapes=turned_scratch(*weights),
        ),
        out_shape=jax.ShapeDtypeStruct((steps, width, size), jnp.bfloat16),
        name="voxel_block",
    )(counts, feat, *weights)


def pool_kernel(
    n_tile,
    n_band,
    cell_ref,
    enc_ref,
    grid_ref,
    low_ref,
    high_ref,
    acc,
    mine,
    theirs,
    came,
    ready,
    landed,
    low,
    high,
    swap_send,
    swap_recv,
    send,
    recv,
    halo_send,
    halo_recv,
):
    tile = lax.axis_index("tile")
    band = lax.axis_index("band")
    other = 1 - band
    strip = tile * n_band + band
    chunks, width, size = enc_ref.shape
    blocks = mine.shape[0]
    per = n_tile // blocks
    cells = WSIDE * CB
    block = acc.shape[0]
    mesh_id = pl.DeviceIdType.MESH

    def strip_id(s):
        return (s // n_band, s % n_band)

    barrier = pltpu.get_barrier_semaphore()

    def greet(i, carry):
        peer = lax.rem(tile + i, n_tile)
        pl.semaphore_signal(barrier, inc=1, device_id=(peer, band), device_id_type=mesh_id)
        return carry

    lax.fori_loop(1, n_tile, greet, 0)
    pl.semaphore_signal(barrier, inc=1, device_id=(tile, other), device_id_type=mesh_id)
    across_below = jnp.logical_and(band == 0, tile > 0)
    across_above = jnp.logical_and(band == n_band - 1, tile < n_tile - 1)

    @pl.when(across_below)
    def _():
        pl.semaphore_signal(barrier, inc=1, device_id=strip_id(strip - 1), device_id_type=mesh_id)

    @pl.when(across_above)
    def _():
        pl.semaphore_signal(barrier, inc=1, device_id=strip_id(strip + 1), device_id_type=mesh_id)

    across = jnp.logical_or(across_below, across_above)

    @pl.when(across)
    def _():
        pl.semaphore_wait(barrier, n_tile + 1)

    @pl.when(jnp.logical_not(across))
    def _():
        pl.semaphore_wait(barrier, n_tile)

    row = lax.broadcasted_iota(jnp.int32, (block, size), 0)

    def place(i):
        return lax.rem(tile // per + 1 + i, blocks)

    def swap(j):
        return pltpu.make_async_remote_copy(
            src_ref=theirs.at[j],
            dst_ref=came.at[j],
            send_sem=swap_send.at[j],
            recv_sem=swap_recv.at[j],
            device_id=(tile, other),
            device_id_type=mesh_id,
        )

    def deliver(dest, source):
        return pltpu.make_async_remote_copy(
            src_ref=ready.at[dest],
            dst_ref=landed.at[source],
            send_sem=send.at[dest],
            recv_sem=recv.at[source],
            device_id=(dest, band),
            device_id_type=mesh_id,
        )

    def compute(i):
        j = place(i)
        acc[...] = jnp.zeros_like(acc)
        together = 2 if chunks % 2 == 0 else 1

        def add(c, carry):
            term = None
            for k in range(together):
                hot = jnp.where(row == cell_ref[together * c + k] - j * block, 1.0, 0.0)
                part = dot(hot.astype(jnp.bfloat16), enc_ref[together * c + k], (1, 1))
                term = part if term is None else term + part
            acc[...] += term
            return carry

        lax.fori_loop(0, chunks // together, add, 0)
        for d in range(per):
            at = d * n_band * cells
            mine[j, d * cells : (d + 1) * cells, :] = acc[
                pl.ds(pl.multiple_of(at + band * cells, cells), cells), :
            ].astype(jnp.bfloat16)
            theirs[j, d * cells : (d + 1) * cells, :] = acc[
                pl.ds(pl.multiple_of(at + other * cells, cells), cells), :
            ].astype(jnp.bfloat16)
        swap(j).start()

    def finish(i):
        j = place(i)
        swap(j).wait_recv()
        total = mine[j].astype(jnp.float32) + came[j].astype(jnp.float32)
        normal = layer_norm(total).reshape(per, WSIDE, CB, width).astype(jnp.bfloat16)
        for d in range(per):
            dest = j * per + d

            @pl.when(dest != tile)
            def _():
                ready[dest] = normal[d]
                deliver(dest, tile).start()

            @pl.when(dest == tile)
            def _():
                landed[tile] = normal[d]

    compute(0)

    def both(i, carry):
        compute(i)
        finish(i - 1)
        return carry

    lax.fori_loop(1, blocks, both, 0)
    finish(blocks - 1)

    def arrive(i, carry):
        peer = lax.rem(tile + i, n_tile)
        deliver(peer, peer).wait_recv()
        return carry

    lax.fori_loop(1, n_tile, arrive, 0)

    def edge(side, target):
        return pltpu.make_async_remote_copy(
            src_ref=landed.at[:, 0 if side == 0 else WSIDE - 1],
            dst_ref=high if side == 0 else low,
            send_sem=halo_send.at[side],
            recv_sem=halo_recv.at[side],
            device_id=strip_id(target),
            device_id_type=mesh_id,
        )

    has_below = strip > 0
    has_above = strip < n_tile * n_band - 1

    @pl.when(has_below)
    def _():
        edge(0, strip - 1).start()

    @pl.when(has_above)
    def _():
        edge(1, strip + 1).start()

    grid_ref[...] = landed[...]

    def left(i, carry):
        peer = lax.rem(tile + i, n_tile)
        deliver(peer, peer).wait_send()
        return carry

    lax.fori_loop(1, n_tile, left, 0)

    def swapped(j, carry):
        swap(j).wait_send()
        return carry

    lax.fori_loop(0, blocks, swapped, 0)

    @pl.when(has_below)
    def _():
        edge(0, strip - 1).wait_send()
        edge(1, strip - 1).wait_recv()
        low_ref[...] = low[...]

    @pl.when(has_above)
    def _():
        edge(1, strip + 1).wait_send()
        edge(0, strip + 1).wait_recv()
        high_ref[...] = high[...]

    @pl.when(strip == 0)
    def _():
        low_ref[...] = jnp.zeros_like(low_ref)

    @pl.when(strip == n_tile * n_band - 1)
    def _():
        high_ref[...] = jnp.zeros_like(high_ref)


def pool_exchange(encoded, target, n_tile, n_band):
    chunks, width, size = encoded.shape
    cells = WSIDE * CB
    per = 2 if n_tile % 2 == 0 else 1
    blocks = n_tile // per
    half = jnp.bfloat16
    vmem = pl.BlockSpec(memory_space=pltpu.VMEM)
    return pl.pallas_call(
        functools.partial(pool_kernel, n_tile, n_band),
        in_specs=[vmem] * 2,
        out_specs=[vmem] * 3,
        out_shape=[
            jax.ShapeDtypeStruct((n_tile, WSIDE, CB, width), half),
            jax.ShapeDtypeStruct((n_tile, CB, width), half),
            jax.ShapeDtypeStruct((n_tile, CB, width), half),
        ],
        scratch_shapes=[
            pltpu.VMEM((per * n_band * cells, width), jnp.float32),
            pltpu.VMEM((blocks, per * cells, width), half),
            pltpu.VMEM((blocks, per * cells, width), half),
            pltpu.VMEM((blocks, per * cells, width), half),
            pltpu.VMEM((n_tile, WSIDE, CB, width), half),
            pltpu.VMEM((n_tile, WSIDE, CB, width), half),
            pltpu.VMEM((n_tile, CB, width), half),
            pltpu.VMEM((n_tile, CB, width), half),
            pltpu.SemaphoreType.DMA((blocks,)),
            pltpu.SemaphoreType.DMA((blocks,)),
            pltpu.SemaphoreType.DMA((n_tile,)),
            pltpu.SemaphoreType.DMA((n_tile,)),
            pltpu.SemaphoreType.DMA((2,)),
            pltpu.SemaphoreType.DMA((2,)),
        ],
        compiler_params=pltpu.CompilerParams(collective_id=0, has_side_effects=True),
        name="pool_exchange",
    )(target.reshape(chunks, 1, size), encoded)


def bev_kernel(
    grid_ref,
    low_ref,
    high_ref,
    tap_ref,
    qkv_ref,
    out_ref,
    up_ref,
    down_ref,
    result_ref,
    wide,
    qv_s,
    out_s,
    up_s,
    down_s,
):
    step = pl.program_id(0)
    n_tile, _, _, width = grid_ref.shape
    span = result_ref.shape[1]

    @pl.when(step == 0)
    def _():
        turn_weights(qkv_ref, out_ref, up_ref, down_ref, qv_s, out_s, up_s, down_s)
        edge = jnp.zeros((WSIDE + 2, CB, width), jnp.float32)
        wide[:, :CB, :] = edge
        wide[:, (n_tile + 1) * CB :, :] = edge

        def fill(t, carry):
            to = pl.ds(pl.multiple_of((t + 1) * CB, CB), CB)
            wide[0, to, :] = low_ref[t].astype(jnp.float32)
            wide[WSIDE + 1, to, :] = high_ref[t].astype(jnp.float32)
            wide[1 : WSIDE + 1, to, :] = grid_ref[t].astype(jnp.float32)
            return carry

        lax.fori_loop(0, n_tile, fill, 0)

    at = pl.multiple_of(step * span, span)
    sums = [jnp.zeros((span, width), jnp.float32) for _ in range(WSIDE)]
    centers = []
    for r in range(WSIDE + 2):
        slab = wide[r, pl.ds(at, span + 2 * CB), :]
        for c in range(3):
            moved = slab[CB + c - 1 : CB + c - 1 + span]
            if c == 1:
                centers.append(moved)
            for row_tap in range(3):
                to = r - row_tap
                if 0 <= to < WSIDE:
                    tap = tap_ref[3 * row_tap + c : 3 * row_tap + c + 1, :]
                    sums[to] = sums[to] + moved * tap
    shaped = [centers[r + 1] + sums[r] for r in range(WSIDE)]
    count = span // CB
    x = jnp.concatenate(
        [shaped[r][w * CB : (w + 1) * CB] for w in range(count) for r in range(WSIDE)], axis=0
    ).astype(jnp.bfloat16)
    result = attend_columns(
        x, None, qv_s[...], qkv_ref[:, width : 2 * width], out_s[...], up_s[...], down_s[...]
    ).T
    for r in range(WSIDE):
        result_ref[r] = jnp.concatenate(
            [result[(w * WSIDE + r) * CB : (w * WSIDE + r + 1) * CB] for w in range(count)], axis=0
        ).astype(jnp.bfloat16)


def bev_block(grid, low, high, taps, weights):
    n_tile, _, _, width = grid.shape
    cols = n_tile * CB
    span = min(64, cols)
    inputs = (grid, low, high, taps, *weights)
    return pl.pallas_call(
        bev_kernel,
        grid=(cols // span,),
        in_specs=[whole(a) for a in inputs],
        out_specs=pl.BlockSpec((WSIDE, span, width), lambda i: (0, i, 0)),
        out_shape=jax.ShapeDtypeStruct((WSIDE, cols, width), jnp.bfloat16),
        scratch_shapes=[pltpu.VMEM((WSIDE + 2, cols + 2 * CB, width), jnp.float32)]
        + turned_scratch(*weights),
        name="bev_block",
    )(*inputs)


def shards(
    voxel_feat,
    window_count,
    voxel_cell,
    w_qkv_voxel,
    w_out_voxel,
    w_up_voxel,
    w_down_voxel,
    conv_taps,
    w_qkv_bev,
    w_out_bev,
    w_up_bev,
    w_down_bev,
):
    n_tile = lax.axis_size("tile")
    n_band = lax.axis_size("band")
    width = voxel_feat.shape[2]
    slot_ids = jnp.arange(voxel_feat.shape[1], dtype=jnp.int32)
    keep = slot_ids[None, :] < window_count[:, None]
    target = jnp.where(keep, voxel_cell, -1)
    encoded = voxel_block(
        voxel_feat.reshape(-1, width),
        window_count,
        (w_qkv_voxel, w_out_voxel, w_up_voxel, w_down_voxel),
    )
    grid, low, high = pool_exchange(encoded, target, n_tile, n_band)
    return bev_block(
        grid, low, high, conv_taps, (w_qkv_bev, w_out_bev, w_up_bev, w_down_bev)
    )


def solution(mesh):
    placed = (
        P(("tile", "band"), None, None),
        P(("tile", "band")),
        P(("tile", "band"), None),
        P(),
        P(),
        P(),
        P(),
        P(),
        P(),
        P(),
        P(),
        P(),
    )
    return jax.shard_map(
        shards,
        mesh=mesh,
        in_specs=placed,
        out_specs=P(("tile", "band"), None, None),
        check_vma=False,
    )
```

time: 127 us -> 87.7 us (0.69); the launches traced: 125 us -> 87.4 us
  starting transfers between devices: 15.3 us -> 0 us
  waiting for transfers between devices: 14 us -> 0 us
  local copies, waits for them, and re-layouts: 12.6 us -> 0.81 us
  Pallas kernels: 78.6 us -> 85.8 us
  other arithmetic: 4.25 us -> 0.77 us
    all_to_all x1 -> x0, waiting for transfers between devices: 9.19 us -> none  [shards(): lax.all_to_all(strip_part, 'tile', split_axis=0, concat_axis=2, tiled=True)]
    all_to_all x1 -> x0, starting transfers between devices: 7.83 us -> none  [shards(): lax.all_to_all(strip_part, 'tile', split_axis=0, concat_axis=2, tiled=True)]
    ppermute x3 -> x0, starting transfers between devices: 7.48 us -> none  [the longest x1 5.49 us: with_halo(): lax.ppermute(lax.slice_in_dim(block, block.shape[dim] - width, None, axis...]
    pallas_call x2 -> x3, Pallas kernels: 78.6 us -> 85.8 us  [the longest x1 40.2 us: pool_exchange(): pl.pallas_call(functools.partial(pool_kernel, n_tile, n_band), in_specs=[...]
    unnamed x32 -> x0, local copies, waits for them, and re-layouts: 5.41 us -> none
    ppermute x3 -> x0, waiting for transfers between devices: 4.82 us -> none  [the longest x1 2.92 us: with_halo(): lax.ppermute(lax.slice_in_dim(block, 0, width, axis=dim), axis, backward)]
    transpose x2 -> x0, local copies, waits for them, and re-layouts: 2.71 us -> none  [the longest x1 1.87 us: shards(): return result.reshape(across, WSIDE, WSIDE, width).transpose(1, 0, 2, 3)....]
    slice x4 -> x0, local copies, waits for them, and re-layouts: 2.46 us -> none  [the longest x2 2.44 us: turned_weights(): return (w_qv, w_qkv[:, width:2 * width], w_out.T, w_up.T, w_down.T)]
  transfers between devices with their start and end apart: 4 -> 0, of which waited for: 3 -> 0; matrix products, arithmetic and copies ran while one was open for 3% -> 0% of each run, Pallas kernels for 0% -> 0%
where the time goes in v1:
time: 87.7 us; the launch traced here: 87.4 us
  Pallas kernels  85.8 us (98%)
    pallas_call x1, Pallas kernels, pool_exchange(): pl.pallas_call(functools.partial(pool_kernel, n_tile, n_band), in_specs=[...  40.2 us
    pallas_call x1, Pallas kernels, voxel_block(): pl.pallas_call(voxel_kernel, grid_spec=pltpu.PrefetchScalarGridSpec(num_s...  37.4 us
    pallas_call x1, Pallas kernels, bev_block(): pl.pallas_call(bev_kernel, grid=(cols // span,), in_specs=[whole(a) for a...  8.19 us

profile of v1, /device:TPU:1, one launch (start us, length us, event | category | flops | bytes accessed | tf_op | source)
XLA Modules:
  0.0 87.4 jit_solution(4266679582908383685)
XLA Ops:
  0.0 0.8 fusion
  0.8 0.1 copy.14
  0.9 0.7 reshape.9.cell_ref
  1.6 37.4 %voxel_block.1.enc_ref = bf16[16,256,512]{2,1,0:T(8,128)(2,1)} custom-call(s32[128]{0:T(128)} %count_ref.1, bf16[8192,256]{1,0:T(8,128)(2,1)} %bitcast.1, bf16[256,768]{1,0:T(8,128)(2,1)} %qkv_ref.2, bf16[256,256]{1,0:T(8,128)(2,1)} %out_ref.2, bf16[256,512]{1,0:T(8,128)(2,1)} %up_ref.2, bf16[512,256]{1,0:T(8,128)(2,1)} %down_ref.2), custom_call_target="tpu_custom_call" | custom-call | tf_op jit(solution)/shard_map/voxel_block/pallas_call | solution.py:154
  39.0 40.2 %pool_exchange.1 = (bf16[16,8,8,256]{3,2,1,0:T(8,128)(2,1)}, bf16[16,8,256]{2,1,0:T(8,128)(2,1)}, bf16[16,8,256]{2,1,0:T(8,128)(2,1)}) custom-call(s32[16,1,512]{2,1,0:T(1,128)} %reshape.9.cell_ref, bf16[16,256,512]{2,1,0:T(8,128)(2,1)} %voxel_block.1.enc_ref), custom_call_target="tpu_custom_call" | custom-call | tf_op jit(solution)/shard_map/pool_exchange/pallas_call | solution.py:384
  79.2 8.2 %bev_block.1 = bf16[8,128,256]{2,1,0:T(8,128)(2,1)} custom-call(bf16[16,8,8,256]{3,2,1,0:T(8,128)(2,1)} %get-tuple-element.8.grid_ref, bf16[16,8,256]{2,1,0:T(8,128)(2,1)} %get-tuple-element.9.low_ref, bf16[16,8,256]{2,1,0:T(8,128)(2,1)} %get-tuple-element.10.high_ref, f32[9,256]{1,0:T(8,128)} %tap_ref.1, bf16[256,768]{1,0:T(8,128)(2,1)} %qkv_ref.3, ...), custom_call_target="tpu_custom_call" | custom-call | tf_op jit(solution)/shard_map/bev_block/pallas_call | solution.py:483

commit v2 on v1

--- a/solution.py
+++ b/solution.py
@@ -43,10 +43,7 @@
     second_b = 1 - first_b
     key_head = lane[:slots] // head_dim
     key_masks = [(key_head == h).astype(jnp.bfloat16) for h in range(half_heads)]
-    val_masks = [
-        (row // head_dim == 2 * j + lane // slots).astype(jnp.bfloat16)
-        for j in range(half_heads // 2)
-    ]
+    val_masks = [(row // head_dim == h).astype(jnp.bfloat16) for h in range(half_heads)]
     mixed = []
     for pair in range(tokens // LANES):
         at = pair * LANES
@@ -78,15 +75,17 @@
             raised = jnp.exp2((scores - top) * factor)
             total = jnp.sum(raised, axis=1, keepdims=True)
             weights = raised.astype(jnp.bfloat16).reshape(half_heads * slots, LANES)
-            v = vals[f : f + LANES, at : at + LANES]
-            rolled = pltpu.roll(v, slots, 1)
-            v_blocks = []
-            for w in range(2):
-                twice = (jnp.where(first, v, rolled) if w == 0 else jnp.where(first, rolled, v))
-                twice = twice.astype(jnp.bfloat16)
-                v_blocks.append(jnp.concatenate([twice * m for m in val_masks], axis=1))
-            out = dot(jnp.concatenate(v_blocks, axis=0), weights)
-            out = jnp.where(first, out[:LANES], out[LANES:])
+            v = vals[f : f + LANES, at : at + LANES].astype(jnp.bfloat16)
+            v_blocks = jnp.concatenate([v * m for m in val_masks], axis=1)
+            spread = jnp.concatenate(
+                [
+                    weights[h * slots : (h + 1) * slots] * m
+                    for h in range(half_heads)
+                    for m in (first_b[:slots], second_b[:slots])
+                ],
+                axis=0,
+            )
+            out = dot(v_blocks, spread)
             out = out.reshape(half_heads, head_dim, LANES) / total
             halves.append(out.reshape(LANES, LANES).astype(jnp.bfloat16))
         mixed.append(jnp.concatenate(halves, axis=0))
@@ -136,7 +135,7 @@
     def _():
         turn_weights(qkv_ref, out_ref, up_ref, down_ref, qv_s, out_s, up_s, down_s)
 
-    enc_ref[0] = attend_columns(
+    enc_ref[...] = attend_columns(
         x_ref[...],
         lambda w: count_ref[step * per_step + w],
         qv_s[...],
@@ -144,7 +143,7 @@
         out_s[...],
         up_s[...],
         down_s[...],
-    ).astype(jnp.bfloat16)
+    ).T.astype(jnp.bfloat16)
 
 
 def voxel_block(feat, counts, weights):
@@ -158,10 +157,10 @@
             grid=(steps,),
             in_specs=[pl.BlockSpec((size, width), lambda i, c: (i, 0))]
             + [whole(w) for w in weights],
-            out_specs=pl.BlockSpec((1, width, size), lambda i, c: (i, 0, 0)),
+            out_specs=pl.BlockSpec((size, width), lambda i, c: (i, 0)),
             scratch_shapes=turned_scratch(*weights),
         ),
-        out_shape=jax.ShapeDtypeStruct((steps, width, size), jnp.bfloat16),
+        out_shape=jax.ShapeDtypeStruct((tokens, width), jnp.bfloat16),
         name="voxel_block",
     )(counts, feat, *weights)
 
@@ -193,7 +192,8 @@
     band = lax.axis_index("band")
     other = 1 - band
     strip = tile * n_band + band
-    chunks, width, size = enc_ref.shape
+    chunks, _, size = cell_ref.shape
+    width = enc_ref.shape[1]
     blocks = mine.shape[0]
     per = n_tile // blocks
     cells = WSIDE * CB
@@ -236,7 +236,8 @@
     row = lax.broadcasted_iota(jnp.int32, (block, size), 0)
 
     def place(i):
-        return lax.rem(tile // per + 1 + i, blocks)
+        ahead = jnp.where(i < blocks - blocks // 2, blocks // 2 + i, blocks - 1 - i)
+        return lax.rem(tile // per + ahead, blocks)
 
     def swap(j):
         return pltpu.make_async_remote_copy(
@@ -261,13 +262,14 @@
     def compute(i):
         j = place(i)
         acc[...] = jnp.zeros_like(acc)
-        together = 2 if chunks % 2 == 0 else 1
+        together = math.gcd(chunks, 8)
 
         def add(c, carry):
             term = None
             for k in range(together):
                 hot = jnp.where(row == cell_ref[together * c + k] - j * block, 1.0, 0.0)
-                part = dot(hot.astype(jnp.bfloat16), enc_ref[together * c + k], (1, 1))
+                at = pl.multiple_of((together * c + k) * size, size)
+                part = dot(hot.astype(jnp.bfloat16), enc_ref[pl.ds(at, size), :])
                 term = part if term is None else term + part
             acc[...] += term
             return carry
@@ -375,9 +377,11 @@
 
 
 def pool_exchange(encoded, target, n_tile, n_band):
-    chunks, width, size = encoded.shape
+    tokens, width = encoded.shape
+    size = min(512, tokens)
+    chunks = tokens // size
     cells = WSIDE * CB
-    per = 2 if n_tile % 2 == 0 else 1
+    per = math.gcd(n_tile, 4)
     blocks = n_tile // per
     half = jnp.bfloat16
     vmem = pl.BlockSpec(memory_space=pltpu.VMEM)

time: 87.7 us -> 78.5 us (0.90)
  Pallas kernels: 85.8 us -> 76.2 us
    pallas_call x1, Pallas kernels: 40.2 us -> 29.9 us  [pool_exchange(): pl.pallas_call(functools.partial(pool_kernel, n_tile, n_band), in_specs=[...]
where the time goes in v2:
time: 78.5 us; the launch traced here: 77.8 us
  Pallas kernels  76.2 us (97%)
  local copies, waits for them, and re-layouts  0.81 us (1%)
    pallas_call x1, Pallas kernels, voxel_block(): pl.pallas_call(voxel_kernel, grid_spec=pltpu.PrefetchScalarGridSpec(num_s...  38.3 us
    pallas_call x1, Pallas kernels, pool_exchange(): pl.pallas_call(functools.partial(pool_kernel, n_tile, n_band), in_specs=[...  29.9 us
    pallas_call x1, Pallas kernels, bev_block(): pl.pallas_call(bev_kernel, grid=(cols // span,), in_specs=[whole(a) for a...  8.06 us

profile of v2, /device:TPU:1, one launch (start us, length us, event | category | flops | bytes accessed | tf_op | source)
XLA Modules:
  0.0 77.8 jit_solution(12502084813596541040)
XLA Ops:
  0.0 0.8 fusion
  0.8 0.1 copy.14
  0.9 0.7 reshape.9.cell_ref
  1.6 38.3 %voxel_block.1.enc_ref = bf16[8192,256]{1,0:T(8,128)(2,1)} custom-call(s32[128]{0:T(128)} %count_ref.1, bf16[8192,256]{1,0:T(8,128)(2,1)} %bitcast.1, bf16[256,768]{1,0:T(8,128)(2,1)} %qkv_ref.2, bf16[256,256]{1,0:T(8,128)(2,1)} %out_ref.2, bf16[256,512]{1,0:T(8,128)(2,1)} %up_ref.2, bf16[512,256]{1,0:T(8,128)(2,1)} %down_ref.2), custom_call_target="tpu_custom_call" | custom-call | tf_op jit(solution)/shard_map/voxel_block/pallas_call | solution.py:153
  39.8 29.9 %pool_exchange.1 = (bf16[16,8,8,256]{3,2,1,0:T(8,128)(2,1)}, bf16[16,8,256]{2,1,0:T(8,128)(2,1)}, bf16[16,8,256]{2,1,0:T(8,128)(2,1)}) custom-call(s32[16,1,512]{2,1,0:T(1,128)} %reshape.9.cell_ref, bf16[8192,256]{1,0:T(8,128)(2,1)} %voxel_block.1.enc_ref), custom_call_target="tpu_custom_call" | custom-call | tf_op jit(solution)/shard_map/pool_exchange/pallas_call | solution.py:388
  69.7 8.1 %bev_block.1 = bf16[8,128,256]{2,1,0:T(8,128)(2,1)} custom-call(bf16[16,8,8,256]{3,2,1,0:T(8,128)(2,1)} %get-tuple-element.8.grid_ref, bf16[16,8,256]{2,1,0:T(8,128)(2,1)} %get-tuple-element.9.low_ref, bf16[16,8,256]{2,1,0:T(8,128)(2,1)} %get-tuple-element.10.high_ref, f32[9,256]{1,0:T(8,128)} %tap_ref.1, bf16[256,768]{1,0:T(8,128)(2,1)} %qkv_ref.3, ...), custom_call_target="tpu_custom_call" | custom-call | tf_op jit(solution)/shard_map/bev_block/pallas_call | solution.py:487
